TPU v7x, 32 devices: a whole 2x2x4 slice. The times are simulated.
32 devices in a mesh: seq: 2 (over x), tok: 16 (over z, y, core).
Axes of the slice: x: 2, y: 2, z: 4, core: 2. Of those that a mesh axis runs over, the one named last changes fastest.
Arguments:
- queries: bfloat16 [8192, 4096], P(('seq', 'tok')), parts along dimension 0, may hold values from -6 to 6
- keys: bfloat16 [8192, 4096], P(('seq', 'tok')), parts along dimension 0, may hold values from -6 to 6
- values: bfloat16 [8192, 4096], P(('seq', 'tok')), parts along dimension 0, may hold values from -6 to 6
- segments: int32 [8192], P(('seq', 'tok')), parts along dimension 0, may hold values from 0 to 31, never falling along the last dimension, each value on 1 to 256 neighbouring positions
- short_filters: bfloat16 [3, 3, 4096], replicated, may hold values from -3.5 to 3.5
- mr_filter: bfloat16 [128, 256], replicated, may hold values from -0.5 to 0.5
- mr_bias: bfloat16 [4096], replicated, may hold values from -1 to 1
Outputs:
- mixed: bfloat16 [8192, 4096], P(('seq', 'tok')), parts along dimension 0
There are 2 independent parts, one for each index of `seq`. A program takes and returns all parts, laid end to end along the dimension named above; an argument that names none is the same for every part. Nothing has to cross between parts.
Inputs may be any that keep to these rules, and one draw needn't show every extreme that they name: `segments`: document numbers never fall along the window; each document spans 1 to 256 positions, and one spans exactly 256.
All inputs are finite; a program needn't handle non-finite values.
Results may differ from a plain program's by a relative error of at most 0.0049.
Values may be sent and summed in bfloat16 or wider, within the bound.
A program may use at most 128 MiB of HBM per device.

v0:
```python
import functools

import jax
import jax.numpy as jnp
from jax import lax
from jax.experimental import pallas as pl
from jax.experimental.pallas import tpu as pltpu
from jax.sharding import PartitionSpec as P

LANES = 128
TILE = 512
F32, BF16 = jnp.float32, jnp.bfloat16


def column(row, block):
    return jnp.transpose(jnp.broadcast_to(row, (block, block)))


def feature(x, before, taps, one, two):
    x = x.astype(F32)
    at = lax.broadcasted_iota(jnp.int32, x.shape, 0)
    far, near = before[0:1], before[1:2]
    x1 = jnp.where(at == 0, near, pltpu.roll(x, 1, 0))
    x2 = jnp.where(at == 0, far, jnp.where(at == 1, near, pltpu.roll(x, 2, 0)))
    return taps[0:1] * x + (taps[1:2] * x1) * one + (taps[2:3] * x2) * two


def kernel(axis, members, tiles, q, k, v, seg_hbm, taps_hbm, filters_hbm, bias_hbm, out,
           seg, taps, filters, bias, qb, kb, vb, pt, halo, raw, edge_send, edge, seg_prev, hrev, biasf,
           table0, table1, picked, masks, shorts,
           small_sem, raw_sem, tail_sem, head_sem, q_sem,
           send_sem, recv_sem, small_send, small_recv):
    rows, width = q.shape
    block = filters.shape[0]
    tile = width // tiles
    per = LANES // members
    keep = block - 16
    me = lax.axis_index(axis)
    size = lax.axis_size(axis)
    has_left, has_right = me > 0, me < size - 1
    left, right = jnp.maximum(me - 1, 0), jnp.minimum(me + 1, size - 1)
    barrier = pltpu.get_barrier_semaphore()

    @pl.when(has_left)
    def _():
        pl.semaphore_signal(barrier, inc=1, device_id={axis: left}, device_id_type=pl.DeviceIdType.MESH)

    @pl.when(has_right)
    def _():
        pl.semaphore_signal(barrier, inc=1, device_id={axis: right}, device_id_type=pl.DeviceIdType.MESH)

    def cols(c):
        return pl.ds(pl.multiple_of(c * tile, tile), tile)

    def raw_copy(i):
        return pltpu.make_async_copy((q, k, v)[i].at[pl.ds(rows - 8, 8)], raw.at[i], raw_sem.at[i])

    def tail_copy(i, c):
        at = pl.ds(keep, rows - keep)
        return pltpu.make_async_copy(
            (k, v)[i].at[at, cols(c)], (kb, vb)[i].at[c, at], tail_sem.at[i, c])

    def head_copy(i, c):
        at = pl.ds(0, keep)
        return pltpu.make_async_copy(
            (k, v)[i].at[at, cols(c)], (kb, vb)[i].at[c, at], head_sem.at[i, c])

    def q_copy(c):
        return pltpu.make_async_copy(q.at[:, cols(c)], qb.at[c], q_sem.at[c])

    def remote(src, dst, s, r):
        return pltpu.make_async_remote_copy(
            src_ref=src, dst_ref=dst, send_sem=s, recv_sem=r,
            device_id={axis: right}, device_id_type=pl.DeviceIdType.MESH)

    def product_copy(c):
        return remote(pt.at[c], halo.at[c], send_sem.at[c], recv_sem.at[c])

    def edge_copy():
        return remote(edge_send, edge, small_send.at[0], small_recv.at[0])

    def seg_copy():
        return remote(seg, seg_prev, small_send.at[1], small_recv.at[1])

    small = [
        pltpu.make_async_copy(src, dst, small_sem.at[i])
        for i, (src, dst) in enumerate(
            ((seg_hbm, seg), (taps_hbm, taps), (filters_hbm, filters), (bias_hbm, bias)))
    ]
    small[0].start()
    for i in range(3):
        raw_copy(i).start()
    small[1].start()

    @pl.loop(0, tiles)
    def _(c):
        tail_copy(0, c).start()
        tail_copy(1, c).start()

    small[2].start()
    small[3].start()

    @pl.loop(0, tiles)
    def _(c):
        head_copy(0, c).start()
        head_copy(1, c).start()
        q_copy(c).start()

    tap = lax.broadcasted_iota(jnp.int32, (block, block), 0)
    lane = lax.broadcasted_iota(jnp.int32, (block, block), 1)

    def make_masks(b, row_before, row):
        own, early = column(row, block), column(row_before, block)
        one = jnp.where(tap == 0, pltpu.roll(early, 1, 0), pltpu.roll(own, 1, 0))
        two = jnp.where(tap < 2, pltpu.roll(early, 2, 0), pltpu.roll(own, 2, 0))
        shorts[b, 0] = jnp.where(own == one, 1.0, 0.0)
        shorts[b, 1] = jnp.where(own == two, 1.0, 0.0)
        masks[b, 0] = jnp.where((own == row_before) & (lane > tap), 1.0, 0.0).astype(BF16)
        masks[b, 1] = jnp.where((own == row) & (lane <= tap), 1.0, 0.0).astype(BF16)

    small[0].wait()
    seg0, seg1 = seg[0:1].astype(F32), seg[1:2].astype(F32)
    make_masks(1, seg0, seg1)
    for i in range(3):
        raw_copy(i).wait()
    edge_send[...] = jnp.concatenate(
        [raw[i].astype(F32)[6:8] for i in range(3)] + [jnp.zeros((2, width), F32)]).astype(BF16)
    pl.semaphore_wait(barrier, has_left.astype(jnp.int32) + has_right.astype(jnp.int32))

    @pl.when(has_right)
    def _():
        seg_copy().start()
        edge_copy().start()

    def part(c, s):
        return pl.ds(pl.multiple_of(c * tile + s, LANES), LANES)

    def taps_of(i, at):
        return taps[i, :, at].astype(F32)

    small[1].wait()

    @pl.loop(0, tiles)
    def _(c):
        tail_copy(0, c).wait()
        tail_copy(1, c).wait()
        for s in range(0, tile, LANES):
            at, here = part(c, s), slice(s, s + LANES)
            one, two = shorts[1, 0], shorts[1, 1]
            feats = []
            for i, buf in ((1, kb), (2, vb)):
                before = buf[c, keep:block, here].astype(F32)[14:16]
                feats.append(feature(buf[c, block:, here], before, taps_of(i, at), one, two))
            pt[c, :, here] = (feats[0] * feats[1]).astype(BF16)

        @pl.when(has_right & (c > 0))
        def _():
            product_copy(jnp.maximum(c - 1, 0)).start()

    @pl.when(has_right)
    def _():
        product_copy(tiles - 1).start()

    small[2].wait()
    small[3].wait()
    turn = (tap == lax.rem(block - lane, block)).astype(BF16)
    hrev[...] = lax.dot_general(
        filters[...], turn, (((0,), (0,)), ((), ())), preferred_element_type=F32)
    biasf[...] = bias[...].astype(F32)

    @pl.when(has_left)
    def _():
        seg_copy().wait_recv()
        edge_copy().wait_recv()

    @pl.when(jnp.logical_not(has_left))
    def _():
        seg_prev[...] = jnp.zeros_like(seg_prev)
        edge[...] = jnp.zeros_like(edge)

        @pl.loop(0, tiles)
        def _(c):
            halo[c] = jnp.zeros_like(halo[c])

    make_masks(0, seg_prev[1:2].astype(F32), seg0)
    glane = lane // members

    @pl.loop(0, tiles)
    def _(c):
        head_copy(0, c).wait()
        head_copy(1, c).wait()
        q_copy(c).wait()

        @pl.when(has_left)
        def _():
            product_copy(c).wait_recv()

        for s in range(0, tile, LANES):
            at, here = part(c, s), slice(s, s + LANES)
            edges = edge[:, at].astype(F32)
            one, two = shorts[0, 0], shorts[0, 1]
            fk = feature(kb[c, :block, here], edges[2:4], taps_of(1, at), one, two)
            fv = feature(vb[c, :block, here], edges[4:6], taps_of(2, at), one, two)
            mid = (fk * fv).astype(BF16)
            far, near = halo[c, :, here], pt[c, :, here]
            first = (c * tile + s) // members
            for g in range(per):
                base = jnp.broadcast_to(hrev[pl.ds(first + g, 1), :], (block, block))
                ring = pltpu.roll(base, 0, 1, stride=1, stride_axis=0).astype(BF16)
                here_rows = slice(g * block, (g + 1) * block)
                table0[here_rows, :block] = ring * masks[0, 0]
                table0[here_rows, block:] = ring * masks[0, 1]
                table1[here_rows, :block] = ring * masks[1, 0]
                table1[here_rows, block:] = ring * masks[1, 1]
            brow = biasf[pl.ds((c * tile + s) // LANES, 1), :]
            for b, (table, low, high) in enumerate(((table0, far, mid), (table1, mid, near))):
                every = jnp.dot(table[...], jnp.concatenate([low, high], 0),
                                preferred_element_type=F32)
                for g in range(per):
                    pltpu.store(picked.at[b], every[g * block : (g + 1) * block], mask=glane == g)
                longer = picked[b] + brow * high.astype(F32)
                if b == 0:
                    before = edges[0:2]
                else:
                    before = qb[c, keep:block, here].astype(F32)[14:16]
                own = slice(b * block, (b + 1) * block)
                fq = feature(qb[c, own, here], before, taps_of(0, at), shorts[b, 0], shorts[b, 1])
                out[own, at] = (fq * longer).astype(BF16)

    @pl.when(has_right)
    def _():
        seg_copy().wait_send()
        edge_copy().wait_send()

        @pl.loop(0, tiles)
        def _(c):
            product_copy(c).wait_send()


def per_device(queries, keys, values, segments, short_filters, mr_filter, mr_bias):
    rows, width = queries.shape
    block, groups = mr_filter.shape
    members = width // groups
    tile = min(TILE, width)
    tiles = width // tile
    per = LANES // members
    dma = pltpu.SemaphoreType.DMA
    chunked = lambda r: pltpu.VMEM((tiles, r, tile), BF16)
    return pl.pallas_call(
        functools.partial(kernel, "tok", members, tiles),
        in_specs=[pl.BlockSpec(memory_space=pltpu.HBM)] * 7,
        out_specs=pl.BlockSpec(memory_space=pltpu.VMEM),
        out_shape=pltpu.VMEM((rows, width), BF16),
        scratch_shapes=[
            pltpu.VMEM((rows // block, block), jnp.int32),
            pltpu.VMEM(short_filters.shape, BF16),
            pltpu.VMEM(mr_filter.shape, BF16),
            pltpu.VMEM((width // LANES, LANES), BF16),
            chunked(rows), chunked(rows), chunked(rows),
            chunked(block), chunked(block),
            pltpu.VMEM((3, 8, width), BF16),
            pltpu.VMEM((8, width), BF16),
            pltpu.VMEM((8, width), BF16),
            pltpu.VMEM((rows // block, block), jnp.int32),
            pltpu.VMEM((groups, block), F32),
            pltpu.VMEM((width // LANES, LANES), F32),
            pltpu.VMEM((per * block, 2 * block), BF16),
            pltpu.VMEM((per * block, 2 * block), BF16),
            pltpu.VMEM((2, block, LANES), F32),
            pltpu.VMEM((2, 2, block, block), BF16),
            pltpu.VMEM((2, 2, block, block), F32),
            dma((4,)), dma((3,)), dma((2, tiles)), dma((2, tiles)), dma((tiles,)),
            dma((tiles,)), dma((tiles,)), dma((2,)), dma((2,)),
        ],
        compiler_params=pltpu.CompilerParams(
            collective_id=0, has_side_effects=True, vmem_limit_bytes=28 * 2**20
        ),
    )(*(pltpu.with_memory_space_constraint(x, pltpu.HBM) for x in (
        queries, keys, values, segments.reshape(rows // block, block), short_filters,
        mr_filter, mr_bias.reshape(width // LANES, LANES))))


def solution(mesh):
    placed = (
        P(("seq", "tok"), None),
        P(("seq", "tok"), None),
        P(("seq", "tok"), None),
        P(("seq", "tok")),
        P(),
        P(),
        P(),
    )
    return jax.shard_map(
        per_device, mesh=mesh, in_specs=placed, out_specs=P(("seq", "tok"), None), check_vma=False
    )
```

profile of v0, /device:TPU:16, one launch (start us, length us, event | category | flops | bytes accessed | tf_op | source)
XLA Modules:
  0.0 20.1 jit_solution(5397735979883319380)
XLA Ops:
  0.0 18.8 %shard_map.73 = bf16[256,4096]{1,0:T(8,128)(2,1)S(1)} custom-call(bf16[256,4096]{1,0:T(8,128)(2,1)} %q.1, bf16[256,4096]{1,0:T(8,128)(2,1)} %k.1, bf16[256,4096]{1,0:T(8,128)(2,1)} %v.1, s32[2,128]{1,0:T(2,128)} %bitcast.3, bf16[3,3,4096]{2,1,0:T(4,128)(2,1)} %taps_hbm.1, bf16[128,256]{1,0:T(8,128)(2,1)} %filters_hbm.1, bf16[32,128]{1,0:T(8,128)(2,1)} %bitcast.2), custom_call_target="tpu_custom_call" | custom-call | tf_op jit(solution)/shard_map/pallas_call | solution.py:249
  18.8 1.3 %copy.9 = bf16[256,4096]{1,0:T(8,128)(2,1)} copy(bf16[256,4096]{1,0:T(8,128)(2,1)S(1)} %shard_map.73) | data formatting | bytes 4194304
where the time goes:
time: 20.2 us; the launch traced here: 20.1 us
  Pallas kernels  18.8 us (93%)
  local copies, waits for them, and re-layouts  1.32 us (7%)
    pallas_call x1, Pallas kernels, per_device(): pl.pallas_call(functools.partial(kernel, 'tok', members, tiles), in_specs...  18.8 us
    unnamed x1, local copies, waits for them, and re-layouts  1.32 us

commit v1 on v0

v1 whole, which is shorter than its diff:
```python
import functools

import jax
import jax.numpy as jnp
from jax import lax
from jax.experimental import pallas as pl
from jax.experimental.pallas import tpu as pltpu
from jax.sharding import PartitionSpec as P

LANES = 128
TILE = 512
F32, BF16 = jnp.float32, jnp.bfloat16


def column(row, block):
    return jnp.transpose(jnp.broadcast_to(row, (block, block)))


def kernel(axis, members, tiles, q, k, v, seg_hbm, taps_hbm, filters_hbm, bias_hbm, out,
           seg, taps, filters, bias, qb, kb, vb, pt, halo, raw, edge_send, edge, seg_prev,
           hrev, comb, biasf, segc, one, two, own_head, emask, dmask, tables, gate, rest, wide,
           small_sem, raw_sem, tail_sem, head_sem, q_sem,
           send_sem, recv_sem, small_send, small_recv):
    rows, width = q.shape
    block = filters.shape[0]
    half = block // 2
    tile = width // tiles
    per = LANES // members
    keep = block - 16
    me = lax.axis_index(axis)
    size = lax.axis_size(axis)
    has_left, has_right = me > 0, me < size - 1
    left, right = jnp.maximum(me - 1, 0), jnp.minimum(me + 1, size - 1)
    barrier = pltpu.get_barrier_semaphore()

    @pl.when(has_left)
    def _():
        pl.semaphore_signal(barrier, inc=1, device_id={axis: left}, device_id_type=pl.DeviceIdType.MESH)

    def cols(c):
        return pl.ds(pl.multiple_of(c * tile, tile), tile)

    def raw_copy(i):
        return pltpu.make_async_copy((q, k, v)[i].at[pl.ds(rows - 8, 8)], raw.at[i], raw_sem.at[i])

    def tail_copy(i, c):
        at = pl.ds(keep, rows - keep)
        return pltpu.make_async_copy(
            (k, v)[i].at[at, cols(c)], (kb, vb)[i].at[c, at], tail_sem.at[i, c])

    def head_copy(i, c):
        at = pl.ds(0, keep)
        return pltpu.make_async_copy(
            (k, v)[i].at[at, cols(c)], (kb, vb)[i].at[c, at], head_sem.at[i, c])

    def q_copy(c):
        return pltpu.make_async_copy(q.at[:, cols(c)], qb.at[c], q_sem.at[c])

    def remote(src, dst, s, r):
        return pltpu.make_async_remote_copy(
            src_ref=src, dst_ref=dst, send_sem=s, recv_sem=r,
            device_id={axis: right}, device_id_type=pl.DeviceIdType.MESH)

    def product_copy(c):
        return remote(pt.at[c], halo.at[c], send_sem.at[c], recv_sem.at[c])

    def edge_copy():
        return remote(edge_send, edge, small_send.at[0], small_recv.at[0])

    def seg_copy():
        return remote(seg, seg_prev, small_send.at[1], small_recv.at[1])

    small = [
        pltpu.make_async_copy(src, dst, small_sem.at[i])
        for i, (src, dst) in enumerate(
            ((seg_hbm, seg), (taps_hbm, taps), (filters_hbm, filters), (bias_hbm, bias)))
    ]
    small[0].start()
    for i in range(3):
        raw_copy(i).start()
    small[1].start()

    @pl.loop(0, tiles)
    def _(c):
        tail_copy(0, c).start()
        tail_copy(1, c).start()

    small[2].start()
    small[3].start()

    @pl.loop(0, tiles)
    def _(c):
        head_copy(0, c).start()
        head_copy(1, c).start()
        q_copy(c).start()

    tap = lax.broadcasted_iota(jnp.int32, (half, LANES), 0)
    lane = lax.broadcasted_iota(jnp.int32, (half, LANES), 1)
    strip = lax.broadcasted_iota(jnp.int32, (16, LANES), 1) // members
    pick2 = [(strip % 2 == i).astype(BF16) for i in range(2)]
    pick4 = [(strip % 4 == i).astype(BF16) for i in range(4)]

    def short_masks(at, count):
        here = segc[pl.ds(at + block, count)]
        one[pl.ds(at, count)] = jnp.where(here == segc[pl.ds(at + block - 1, count)], 1.0, 0.0)
        two[pl.ds(at, count)] = jnp.where(here == segc[pl.ds(at + block - 2, count)], 1.0, 0.0)

    def feature(buf, x, lead, taps_rows, at, count):
        buf[pl.ds(lead, x.shape[0])] = x
        first = lead + x.shape[0] - count
        x0 = x[x.shape[0] - count:]
        x1, x2 = buf[pl.ds(first - 1, count)], buf[pl.ds(first - 2, count)]
        return (taps_rows[0:1] * x0 + (taps_rows[1:2] * x1) * one[pl.ds(at, count)]
                + (taps_rows[2:3] * x2) * two[pl.ds(at, count)])

    small[0].wait()
    for b in range(2):
        segc[pl.ds((b + 1) * block, block)] = column(seg[b:b + 1].astype(F32), block)
    short_masks(block, block)
    for i in range(3):
        raw_copy(i).wait()
    edge_send[...] = jnp.concatenate(
        [raw[i].astype(F32)[6:8] for i in range(3)] + [jnp.zeros((2, width), F32)]).astype(BF16)

    @pl.when(has_right)
    def _():
        pl.semaphore_wait(barrier, 1)
        seg_copy().start()
        edge_copy().start()

    def part(c, s):
        return pl.ds(pl.multiple_of(c * tile + s, LANES), LANES)

    def taps_of(i, at):
        return taps[i, :, at].astype(F32)

    small[1].wait()

    @pl.loop(0, tiles)
    def _(c):
        tail_copy(0, c).wait()
        tail_copy(1, c).wait()
        for s in range(0, tile, LANES):
            at, here = part(c, s), slice(s, s + LANES)
            feats = []
            for i, buf in ((1, kb), (2, vb)):
                x = buf[c, keep:, here].astype(F32)
                feats.append(feature(wide.at[i, s // LANES], x, 8, taps_of(i, at), block, block))
            pt[c, :, here] = (feats[0] * feats[1]).astype(BF16)

        @pl.when(has_right)
        def _():
            product_copy(c).start()

    small[2].wait()
    small[3].wait()
    wide_tap = lax.broadcasted_iota(jnp.int32, (block, block), 0)
    wide_lane = lax.broadcasted_iota(jnp.int32, (block, block), 1)
    turn = (wide_tap == lax.rem(block - wide_lane, block)).astype(BF16)
    turned = lax.dot_general(
        filters[...], turn, (((0,), (0,)), ((), ())), preferred_element_type=F32)
    hrev[...] = turned
    groups = turned.shape[0]
    glane = lax.broadcasted_iota(jnp.int32, turned.shape, 1)
    comb[...] = jnp.where((glane >= 1) & (glane <= half),
                          pltpu.roll(pltpu.roll(turned, half, 1), groups - 1, 0), turned)
    biasf[...] = bias[...].astype(F32)

    for b in range(4):
        own = segc[pl.ds(block + b * half, half)]
        start = own[0:1]
        own_head[pl.ds(b * half, half)] = jnp.where(own == start, 1.0, 0.0)
        row = seg[b // 2:b // 2 + 1].astype(F32)
        twin = pltpu.roll(jnp.broadcast_to(row, (8, block)), half, 1)[0:1]
        low = lane[0:1] < half
        row = jnp.where(low, row, twin) if b % 2 == 0 else jnp.where(low, twin, row)
        inner = jnp.where(lane < half, lane, lane - half)
        dmask[b] = jnp.where((own == row) & (inner <= tap), 1.0, 0.0).astype(BF16)

    def early_masks(b):
        start = segc[pl.ds(block + b * half, 8)][0:1]
        same = jnp.where(segc[pl.ds(b * half, block)] == start, 1.0, 0.0).astype(BF16)
        for i in range(2):
            emask[b, i] = same * jnp.concatenate([pick2[i]] * (block // 16), 0)

    early_masks(2)
    early_masks(3)
    later = (lane > tap).astype(BF16)

    @pl.when(has_left)
    def _():
        seg_copy().wait_recv()
        edge_copy().wait_recv()

    @pl.when(jnp.logical_not(has_left))
    def _():
        seg_prev[...] = jnp.zeros_like(seg_prev)
        edge[...] = jnp.zeros_like(edge)

        @pl.loop(0, tiles)
        def _(c):
            halo[c] = jnp.zeros_like(halo[c])

    segc[pl.ds(0, block)] = column(seg_prev[1:2].astype(F32), block)
    short_masks(0, block)
    early_masks(0)
    early_masks(1)

    quad = lax.broadcasted_iota(jnp.int32, (half, LANES), 1) // (2 * members)

    def early(table, low, high, b):
        right_side = jnp.concatenate([
            jnp.concatenate([x * emask[b + j, i] for j, x in enumerate((low, high))], 1)
            for i in range(2)], 0)
        every = jnp.dot(table, right_side, preferred_element_type=F32)
        picked = []
        for j in range(2):
            side = every[:, j * LANES:(j + 1) * LANES]
            parts = [side[h * half:(h + 1) * half] for h in range(4)]
            picked.append(jnp.where(quad == 0, parts[0], jnp.where(
                quad == 1, parts[1], jnp.where(quad == 2, parts[2], parts[3]))))
        return jnp.concatenate(picked, 0)

    @pl.loop(0, tiles)
    def _(c):
        head_copy(0, c).wait()
        head_copy(1, c).wait()
        q_copy(c).wait()
        for s in range(0, tile, LANES):
            at, here, n = part(c, s), slice(s, s + LANES), s // LANES
            edges = edge[:, at].astype(F32)

            def feat(i, buf, count):
                wide[i, n, pl.ds(6, 2)] = edges[2 * i:2 * i + 2]
                return feature(wide.at[i, n], buf[c, :count, here].astype(F32), 8, taps_of(i, at), 0, count)

            mid = (feat(1, kb, block) * feat(2, vb, block)).astype(BF16)
            near = pt[c, :, here]
            first = (c * tile + s) // members

            def ring(source, g):
                base = jnp.broadcast_to(source[pl.ds(first + g, 1), :], (half, block))
                return pltpu.roll(base, 0, 1, stride=1, stride_axis=0).astype(BF16)

            for h in range(4):
                for i in range(2):
                    tables[c, n, h * half:(h + 1) * half, i * block:(i + 1) * block] = ring(hrev, 2 * h + i) * later
            own = [[ring(comb, 4 * h + 2 * i) for i in range(2)] for h in range(2)]
            blocks = (mid[:half], mid[half:], near[:half], near[half:])
            diag = []
            for b in range(4):
                left_side = jnp.concatenate([
                    jnp.concatenate([own[h][i] * dmask[b] for i in range(2)], 1) for h in range(2)], 0)
                right_side = jnp.concatenate([
                    blocks[b] * jnp.concatenate([pick4[i]] * (half // 16), 0) for i in range(4)], 0)
                every = jnp.dot(left_side, right_side, preferred_element_type=F32)
                diag.append(jnp.where(quad < 2, every[:half], every[half:]))
            brow = biasf[pl.ds((c * tile + s) // LANES, 1), :]
            fq = feat(0, qb, rows)
            sure0 = jnp.concatenate(diag[:2], 0) + brow * mid.astype(F32)
            gate[c, n] = fq[:block] * own_head[pl.ds(0, block)]
            rest[c, n] = fq[:block] * sure0
            fresh = early(tables[c, n], mid, jnp.concatenate([mid[half:], near[:half]], 0), 2)
            sure1 = jnp.concatenate(diag[2:], 0) + brow * near.astype(F32)
            out[block:, at] = (fq[block:] * (sure1 + fresh * own_head[pl.ds(block, block)])).astype(BF16)
            kb[c, :half, here] = mid[:half]

    @pl.loop(0, tiles)
    def _(c):
        @pl.when(has_left)
        def _():
            product_copy(c).wait_recv()

        for s in range(0, tile, LANES):
            at, here, n = part(c, s), slice(s, s + LANES), s // LANES
            far = halo[c, :, here]
            fresh = early(tables[c, n], far, jnp.concatenate([far[half:], kb[c, :half, here]], 0), 0)
            out[:block, at] = (gate[c, n] * fresh + rest[c, n]).astype(BF16)

    @pl.when(has_right)
    def _():
        seg_copy().wait_send()
        edge_copy().wait_send()

        @pl.loop(0, tiles)
        def _(c):
            product_copy(c).wait_send()


def per_device(queries, keys, values, segments, short_filters, mr_filter, mr_bias):
    rows, width = queries.shape
    block, groups = mr_filter.shape
    half = block // 2
    members = width // groups
    tile = min(TILE, width)
    tiles = width // tile
    parts = tile // LANES
    dma = pltpu.SemaphoreType.DMA
    chunked = lambda r: pltpu.VMEM((tiles, r, tile), BF16)
    return pl.pallas_call(
        functools.partial(kernel, "tok", members, tiles),
        in_specs=[pl.BlockSpec(memory_space=pltpu.HBM)] * 7,
        out_specs=pl.BlockSpec(memory_space=pltpu.VMEM),
        out_shape=pltpu.VMEM((rows, width), BF16),
        scratch_shapes=[
            pltpu.VMEM((rows // block, block), jnp.int32),
            pltpu.VMEM(short_filters.shape, BF16),
            pltpu.VMEM(mr_filter.shape, BF16),
            pltpu.VMEM((width // LANES, LANES), BF16),
            chunked(rows), chunked(rows), chunked(rows),
            chunked(block), chunked(block),
            pltpu.VMEM((3, 8, width), BF16),
            pltpu.VMEM((8, width), BF16),
            pltpu.VMEM((8, width), BF16),
            pltpu.VMEM((rows // block, block), jnp.int32),
            pltpu.VMEM((groups, block), F32),
            pltpu.VMEM((groups, block), F32),
            pltpu.VMEM((width // LANES, LANES), F32),
            pltpu.VMEM((block + rows, LANES), F32),
            pltpu.VMEM((rows, LANES), F32),
            pltpu.VMEM((rows, LANES), F32),
            pltpu.VMEM((rows, LANES), F32),
            pltpu.VMEM((4, 2, block, LANES), BF16),
            pltpu.VMEM((4, half, LANES), BF16),
            pltpu.VMEM((tiles, parts, 4 * half, 2 * block), BF16),
            pltpu.VMEM((tiles, parts, block, LANES), F32),
            pltpu.VMEM((tiles, parts, block, LANES), F32),
            pltpu.VMEM((3, parts, rows + 8, LANES), F32),
            dma((4,)), dma((3,)), dma((2, tiles)), dma((2, tiles)), dma((tiles,)),
            dma((tiles,)), dma((tiles,)), dma((2,)), dma((2,)),
        ],
        compiler_params=pltpu.CompilerParams(
            collective_id=0, has_side_effects=True, vmem_limit_bytes=40 * 2**20
        ),
    )(*(pltpu.with_memory_space_constraint(x, pltpu.HBM) for x in (
        queries, keys, values, segments.reshape(rows // block, block), short_filters,
        mr_filter, mr_bias.reshape(width // LANES, LANES))))


def solution(mesh):
    placed = (
        P(("seq", "tok"), None),
        P(("seq", "tok"), None),
        P(("seq", "tok"), None),
        P(("seq", "tok")),
        P(),
        P(),
        P(),
    )
    return jax.shard_map(
        per_device, mesh=mesh, in_specs=placed, out_specs=P(("seq", "tok"), None), check_vma=False
    )
```

time: 20.2 us -> 18.3 us (0.906)
  Pallas kernels: 18.8 us -> 16.8 us
    pallas_call x1, Pallas kernels: 18.8 us -> 16.8 us  [per_device(): pl.pallas_call(functools.partial(kernel, 'tok', members, tiles), in_specs...]
where the time goes in v1:
time: 18.3 us; the launch traced here: 18.2 us
  Pallas kernels  16.8 us (92%)
  local copies, waits for them, and re-layouts  1.32 us (7%)
    pallas_call x1, Pallas kernels, per_device(): pl.pallas_call(functools.partial(kernel, 'tok', members, tiles), in_specs...  16.8 us
    unnamed x1, local copies, waits for them, and re-layouts  1.32 us

profile of v1, /device:TPU:16, one launch (start us, length us, event | category | flops | bytes accessed | tf_op | source)
XLA Modules:
  0.0 18.2 jit_solution(17671882913420319845)
XLA Ops:
  0.0 16.8 %shard_map.73 = bf16[256,4096]{1,0:T(8,128)(2,1)S(1)} custom-call(bf16[256,4096]{1,0:T(8,128)(2,1)} %q.1, bf16[256,4096]{1,0:T(8,128)(2,1)} %k.1, bf16[256,4096]{1,0:T(8,128)(2,1)} %v.1, s32[2,128]{1,0:T(2,128)} %bitcast.3, bf16[3,3,4096]{2,1,0:T(4,128)(2,1)} %taps_hbm.1, bf16[128,256]{1,0:T(8,128)(2,1)} %filters_hbm.1, bf16[32,128]{1,0:T(8,128)(2,1)} %bitcast.2), custom_call_target="tpu_custom_call" | custom-call | tf_op jit(solution)/shard_map/pallas_call | solution.py:300
  16.8 1.3 %copy.9 = bf16[256,4096]{1,0:T(8,128)(2,1)} copy(bf16[256,4096]{1,0:T(8,128)(2,1)S(1)} %shard_map.73) | data formatting | bytes 4194304

commit v2 on v1

--- a/solution.py
+++ b/solution.py
@@ -9,6 +9,7 @@
 
 LANES = 128
 TILE = 512
+LAST = 2
 F32, BF16 = jnp.float32, jnp.bfloat16
 
 
@@ -16,9 +17,36 @@
     return jnp.transpose(jnp.broadcast_to(row, (block, block)))
 
 
-def kernel(axis, members, tiles, q, k, v, seg_hbm, taps_hbm, filters_hbm, bias_hbm, out,
-           seg, taps, filters, bias, qb, kb, vb, pt, halo, raw, edge_send, edge, seg_prev,
-           hrev, comb, biasf, segc, one, two, own_head, emask, dmask, tables, gate, rest, wide,
+def quads(half, members):
+    return lax.broadcasted_iota(jnp.int32, (half, LANES), 1) // (2 * members)
+
+
+def early(table, low, high, masks, quad):
+    half = quad.shape[0]
+    right_side = jnp.concatenate([
+        jnp.concatenate([x * masks[j, i] for j, x in enumerate((low, high))], 1)
+        for i in range(2)], 0)
+    every = jnp.dot(table, right_side, preferred_element_type=F32)
+    picked = []
+    for j in range(2):
+        side = every[:, j * LANES:(j + 1) * LANES]
+        parts = [side[h * half:(h + 1) * half] for h in range(4)]
+        picked.append(jnp.where(quad == 0, parts[0], jnp.where(
+            quad == 1, parts[1], jnp.where(quad == 2, parts[2], parts[3]))))
+    return jnp.concatenate(picked, 0)
+
+
+def join(c, n, here, halo, mids, tables, gate, rest, masks, quad):
+    half = quad.shape[0]
+    far = halo[c, :, here]
+    fresh = early(tables[c, n], far, jnp.concatenate([far[half:], mids[c, :, here]], 0), masks, quad)
+    return (gate[c, n] * fresh + rest[c, n]).astype(BF16)
+
+
+def kernel(axis, members, tiles, last, q, k, v, seg_hbm, taps_hbm, filters_hbm, bias_hbm,
+           out, halo, mids, tables, gate, rest, emask,
+           seg, taps, filters, bias, qb, kv, pt, raw, edge_send, edge, seg_prev,
+           hrev, comb, biasf, segc, one, two, own_head, dmask, wide,
            small_sem, raw_sem, tail_sem, head_sem, q_sem,
            send_sem, recv_sem, small_send, small_recv):
     rows, width = q.shape
@@ -41,17 +69,18 @@
         return pl.ds(pl.multiple_of(c * tile, tile), tile)
 
     def raw_copy(i):
-        return pltpu.make_async_copy((q, k, v)[i].at[pl.ds(rows - 8, 8)], raw.at[i], raw_sem.at[i])
+        return pltpu.make_async_copy((q, k, v)[i].at[pl.ds(rows - 8, 8)], raw.at[i], raw_sem.at[0])
 
     def tail_copy(i, c):
         at = pl.ds(keep, rows - keep)
-        return pltpu.make_async_copy(
-            (k, v)[i].at[at, cols(c)], (kb, vb)[i].at[c, at], tail_sem.at[i, c])
+        return pltpu.make_async_copy((k, v)[i].at[at, cols(c)], kv.at[i, c, at], tail_sem.at[c])
 
     def head_copy(i, c):
         at = pl.ds(0, keep)
-        return pltpu.make_async_copy(
-            (k, v)[i].at[at, cols(c)], (kb, vb)[i].at[c, at], head_sem.at[i, c])
+        return pltpu.make_async_copy((k, v)[i].at[at, cols(c)], kv.at[i, c, at], head_sem.at[c])
+
+    def whole(ref, sem):
+        return pltpu.make_async_copy(ref, ref, sem)
 
     def q_copy(c):
         return pltpu.make_async_copy(q.at[:, cols(c)], qb.at[c], q_sem.at[c])
@@ -62,7 +91,7 @@
             device_id={axis: right}, device_id_type=pl.DeviceIdType.MESH)
 
     def product_copy(c):
-        return remote(pt.at[c], halo.at[c], send_sem.at[c], recv_sem.at[c])
+        return remote(pt.at[c], halo.at[c], send_sem.at[0], recv_sem.at[c])
 
     def edge_copy():
         return remote(edge_send, edge, small_send.at[0], small_recv.at[0])
@@ -117,16 +146,9 @@
     for b in range(2):
         segc[pl.ds((b + 1) * block, block)] = column(seg[b:b + 1].astype(F32), block)
     short_masks(block, block)
+    whole(raw, raw_sem.at[0]).wait()
     for i in range(3):
-        raw_copy(i).wait()
-    edge_send[...] = jnp.concatenate(
-        [raw[i].astype(F32)[6:8] for i in range(3)] + [jnp.zeros((2, width), F32)]).astype(BF16)
-
-    @pl.when(has_right)
-    def _():
-        pl.semaphore_wait(barrier, 1)
-        seg_copy().start()
-        edge_copy().start()
+        edge_send[i] = raw[i].astype(F32)[6:8].astype(BF16)
 
     def part(c, s):
         return pl.ds(pl.multiple_of(c * tile + s, LANES), LANES)
@@ -138,15 +160,20 @@
 
     @pl.loop(0, tiles)
     def _(c):
-        tail_copy(0, c).wait()
-        tail_copy(1, c).wait()
+        whole(kv.at[:, c, pl.ds(keep, rows - keep)], tail_sem.at[c]).wait()
         for s in range(0, tile, LANES):
             at, here = part(c, s), slice(s, s + LANES)
             feats = []
-            for i, buf in ((1, kb), (2, vb)):
-                x = buf[c, keep:, here].astype(F32)
+            for i in (1, 2):
+                x = kv[i - 1, c, keep:, here].astype(F32)
                 feats.append(feature(wide.at[i, s // LANES], x, 8, taps_of(i, at), block, block))
             pt[c, :, here] = (feats[0] * feats[1]).astype(BF16)
+
+        @pl.when(has_right & (c == 0))
+        def _():
+            pl.semaphore_wait(barrier, 1)
+            seg_copy().start()
+            edge_copy().start()
 
         @pl.when(has_right)
         def _():
@@ -206,35 +233,20 @@
     early_masks(0)
     early_masks(1)
 
-    quad = lax.broadcasted_iota(jnp.int32, (half, LANES), 1) // (2 * members)
-
-    def early(table, low, high, b):
-        right_side = jnp.concatenate([
-            jnp.concatenate([x * emask[b + j, i] for j, x in enumerate((low, high))], 1)
-            for i in range(2)], 0)
-        every = jnp.dot(table, right_side, preferred_element_type=F32)
-        picked = []
-        for j in range(2):
-            side = every[:, j * LANES:(j + 1) * LANES]
-            parts = [side[h * half:(h + 1) * half] for h in range(4)]
-            picked.append(jnp.where(quad == 0, parts[0], jnp.where(
-                quad == 1, parts[1], jnp.where(quad == 2, parts[2], parts[3]))))
-        return jnp.concatenate(picked, 0)
+    quad = quads(half, members)
 
     @pl.loop(0, tiles)
     def _(c):
-        head_copy(0, c).wait()
-        head_copy(1, c).wait()
+        whole(kv.at[:, c, pl.ds(0, keep)], head_sem.at[c]).wait()
         q_copy(c).wait()
         for s in range(0, tile, LANES):
             at, here, n = part(c, s), slice(s, s + LANES), s // LANES
-            edges = edge[:, at].astype(F32)
-
-            def feat(i, buf, count):
-                wide[i, n, pl.ds(6, 2)] = edges[2 * i:2 * i + 2]
-                return feature(wide.at[i, n], buf[c, :count, here].astype(F32), 8, taps_of(i, at), 0, count)
-
-            mid = (feat(1, kb, block) * feat(2, vb, block)).astype(BF16)
+
+            def feat(i, x):
+                wide[i, n, pl.ds(6, 2)] = edge[i, :, at].astype(F32)
+                return feature(wide.at[i, n], x.astype(F32), 8, taps_of(i, at), 0, x.shape[0])
+
+            mid = (feat(1, kv[0, c, :block, here]) * feat(2, kv[1, c, :block, here])).astype(BF16)
             near = pt[c, :, here]
             first = (c * tile + s) // members
 
@@ -256,35 +268,63 @@
                 every = jnp.dot(left_side, right_side, preferred_element_type=F32)
                 diag.append(jnp.where(quad < 2, every[:half], every[half:]))
             brow = biasf[pl.ds((c * tile + s) // LANES, 1), :]
-            fq = feat(0, qb, rows)
+            fq = feat(0, qb[c, :, here])
             sure0 = jnp.concatenate(diag[:2], 0) + brow * mid.astype(F32)
             gate[c, n] = fq[:block] * own_head[pl.ds(0, block)]
             rest[c, n] = fq[:block] * sure0
-            fresh = early(tables[c, n], mid, jnp.concatenate([mid[half:], near[:half]], 0), 2)
+            fresh = early(tables[c, n], mid, jnp.concatenate([mid[half:], near[:half]], 0), emask.at[2:4], quad)
             sure1 = jnp.concatenate(diag[2:], 0) + brow * near.astype(F32)
             out[block:, at] = (fq[block:] * (sure1 + fresh * own_head[pl.ds(block, block)])).astype(BF16)
-            kb[c, :half, here] = mid[:half]
-
-    @pl.loop(0, tiles)
-    def _(c):
+            mids[c, :, here] = mid[:half]
+
+    def arrive(c):
         @pl.when(has_left)
         def _():
             product_copy(c).wait_recv()
 
+    @pl.loop(0, tiles - last)
+    def _(c):
+        arrive(c)
         for s in range(0, tile, LANES):
-            at, here, n = part(c, s), slice(s, s + LANES), s // LANES
-            far = halo[c, :, here]
-            fresh = early(tables[c, n], far, jnp.concatenate([far[half:], kb[c, :half, here]], 0), 0)
-            out[:block, at] = (gate[c, n] * fresh + rest[c, n]).astype(BF16)
+            out[:block, part(c, s)] = join(
+                c, s // LANES, slice(s, s + LANES), halo, mids, tables, gate, rest, emask.at[0:2], quad)
+
+    @pl.loop(tiles - last, tiles)
+    def _(c):
+        arrive(c)
 
     @pl.when(has_right)
     def _():
         seg_copy().wait_send()
         edge_copy().wait_send()
-
-        @pl.loop(0, tiles)
-        def _(c):
-            product_copy(c).wait_send()
+        remote(pt, halo, send_sem.at[0], recv_sem.at[0]).wait_send()
+
+
+def finish(last, members, done, halo, mids, tables, gate, rest, emask, out, fresh, sem):
+    rows, width = done.shape
+    tiles, block, tile = halo.shape
+    half = mids.shape[1]
+    quad = quads(half, members)
+    ready = width - last * tile
+    copies = [
+        pltpu.make_async_copy(done.at[at], out.at[at], sem.at[i])
+        for i, at in enumerate((
+            (pl.ds(0, block), pl.ds(0, ready)),
+            (pl.ds(block, half), slice(None)),
+            (pl.ds(block + half, half), slice(None))))]
+    for copy in copies:
+        copy.start()
+    for i in range(last):
+        c = tiles - last + i
+        for s in range(0, tile, LANES):
+            here = slice(s, s + LANES)
+            fresh[i, :, here] = join(c, s // LANES, here, halo, mids, tables, gate, rest, emask.at[0:2], quad)
+        copy = pltpu.make_async_copy(
+            fresh.at[i], out.at[pl.ds(0, block), pl.ds(ready + i * tile, tile)], sem.at[3 + i])
+        copy.start()
+        copies.append(copy)
+    for copy in copies:
+        copy.wait()
 
 
 def per_device(queries, keys, values, segments, short_filters, mr_filter, mr_bias):
@@ -297,21 +337,32 @@
     parts = tile // LANES
     dma = pltpu.SemaphoreType.DMA
     chunked = lambda r: pltpu.VMEM((tiles, r, tile), BF16)
-    return pl.pallas_call(
-        functools.partial(kernel, "tok", members, tiles),
+    last = min(LAST, tiles)
+    vmem = pl.BlockSpec(memory_space=pltpu.VMEM)
+    held = pl.pallas_call(
+        functools.partial(kernel, "tok", members, tiles, last),
         in_specs=[pl.BlockSpec(memory_space=pltpu.HBM)] * 7,
-        out_specs=pl.BlockSpec(memory_space=pltpu.VMEM),
-        out_shape=pltpu.VMEM((rows, width), BF16),
+        out_specs=[vmem] * 7,
+        out_shape=[
+            pltpu.VMEM((rows, width), BF16),
+            chunked(block),
+            chunked(half),
+            pltpu.VMEM((tiles, parts, 4 * half, 2 * block), BF16),
+            pltpu.VMEM((tiles, parts, block, LANES), F32),
+            pltpu.VMEM((tiles, parts, block, LANES), F32),
+            pltpu.VMEM((4, 2, block, LANES), BF16),
+        ],
         scratch_shapes=[
             pltpu.VMEM((rows // block, block), jnp.int32),
             pltpu.VMEM(short_filters.shape, BF16),
             pltpu.VMEM(mr_filter.shape, BF16),
             pltpu.VMEM((width // LANES, LANES), BF16),
-            chunked(rows), chunked(rows), chunked(rows),
-            chunked(block), chunked(block),
+            chunked(rows),
+            pltpu.VMEM((2, tiles, rows, tile), BF16),
+            chunked(block),
             pltpu.VMEM((3, 8, width), BF16),
-            pltpu.VMEM((8, width), BF16),
-            pltpu.VMEM((8, width), BF16),
+            pltpu.VMEM((3, 2, width), BF16),
+            pltpu.VMEM((3, 2, width), BF16),
             pltpu.VMEM((rows // block, block), jnp.int32),
             pltpu.VMEM((groups, block), F32),
             pltpu.VMEM((groups, block), F32),
@@ -320,21 +371,25 @@
             pltpu.VMEM((rows, LANES), F32),
             pltpu.VMEM((rows, LANES), F32),
             pltpu.VMEM((rows, LANES), F32),
-            pltpu.VMEM((4, 2, block, LANES), BF16),
             pltpu.VMEM((4, half, LANES), BF16),
-            pltpu.VMEM((tiles, parts, 4 * half, 2 * block), BF16),
-            pltpu.VMEM((tiles, parts, block, LANES), F32),
-            pltpu.VMEM((tiles, parts, block, LANES), F32),
             pltpu.VMEM((3, parts, rows + 8, LANES), F32),
-            dma((4,)), dma((3,)), dma((2, tiles)), dma((2, tiles)), dma((tiles,)),
-            dma((tiles,)), dma((tiles,)), dma((2,)), dma((2,)),
+            dma((4,)), dma((1,)), dma((tiles,)), dma((tiles,)), dma((tiles,)),
+            dma((1,)), dma((tiles,)), dma((2,)), dma((2,)),
         ],
         compiler_params=pltpu.CompilerParams(
-            collective_id=0, has_side_effects=True, vmem_limit_bytes=40 * 2**20
+            collective_id=0, has_side_effects=True, vmem_limit_bytes=24 * 2**20
         ),
     )(*(pltpu.with_memory_space_constraint(x, pltpu.HBM) for x in (
         queries, keys, values, segments.reshape(rows // block, block), short_filters,
         mr_filter, mr_bias.reshape(width // LANES, LANES))))
+    return pl.pallas_call(
+        functools.partial(finish, last, members),
+        in_specs=[vmem] * 7,
+        out_specs=pl.BlockSpec(memory_space=pltpu.HBM),
+        out_shape=pltpu.HBM((rows, width), BF16),
+        scratch_shapes=[pltpu.VMEM((last, block, tile), BF16), dma((3 + last,))],
+        compiler_params=pltpu.CompilerParams(vmem_limit_bytes=8 * 2**20),
+    )(*(pltpu.with_memory_space_constraint(x, pltpu.VMEM) for x in held))
 
 
 def solution(mesh):

time: 18.3 us -> 17.8 us (0.973)
  local copies, waits for them, and re-layouts: 1.32 us -> 0 us
  Pallas kernels: 16.8 us -> 17.6 us
    unnamed x1 -> x0, local copies, waits for them, and re-layouts: 1.32 us -> none
    pallas_call x1 -> x2, Pallas kernels: 16.8 us -> 17.6 us  [the longest x1 16 us: per_device(): pl.pallas_call(functools.partial(kernel, 'tok', members, tiles, last), in...]
where the time goes in v2:
time: 17.8 us; the launch traced here: 17.6 us
  Pallas kernels  17.6 us (99%)
    pallas_call x1, Pallas kernels, per_device(): pl.pallas_call(functools.partial(kernel, 'tok', members, tiles, last), in...  16 us
    pallas_call x1, Pallas kernels, per_device(): pl.pallas_call(functools.partial(finish, last, members), in_specs=[vmem]...  1.57 us

profile of v2, /device:TPU:16, one launch (start us, length us, event | category | flops | bytes accessed | tf_op | source)
XLA Modules:
  0.0 17.6 jit_solution(11998589175043252560)
XLA Ops:
  0.0 16.0 %shard_map.73 = (bf16[256,4096]{1,0:T(8,128)(2,1)S(1)}, bf16[8,128,512]{2,1,0:T(8,128)(2,1)S(1)}, bf16[8,64,512]{2,1,0:T(8,128)(2,1)S(1)}, bf16[8,4,256,256]{3,2...) custom-call(bf16[256,4096]{1,0:T(8,128)(2,1)} %q.1, ...), custom_call_target="tpu_custom_call" | custom-call | tf_op jit(solution)/shard_map/pallas_call | solution.py:342
  16.0 1.6 %shard_map.74 = bf16[256,4096]{1,0:T(8,128)(2,1)} custom-call(bf16[256,4096]{1,0:T(8,128)(2,1)S(1)} %get-tuple-element.12.done, bf16[8,128,512]{2,1,0:T(8,128)(2,1)S(1)} %get-tuple-element.13.halo, bf16[8,64,512]{2,1,0:T(8,128)(2,1)S(1)} %get-tuple-element.14.mids, bf16[8,4,256,256]{3,2,1,0:T(8,128)(2,1)S(1)} %get-tuple-element.15.tables, ...), custom_call_target="tpu_custom_call" | custom-call | tf_op jit(solution)/shard_map/pallas_call | solution.py:385

commit v3 on v2

--- a/solution.py
+++ b/solution.py
@@ -9,7 +9,7 @@
 
 LANES = 128
 TILE = 512
-LAST = 2
+LAST = 3
 F32, BF16 = jnp.float32, jnp.bfloat16
 
 

time: 17.8 us -> 17.6 us (0.989)
  Pallas kernels: 17.6 us -> 17.4 us
    pallas_call x1, Pallas kernels: 1.57 us -> 1.37 us  [per_device(): pl.pallas_call(functools.partial(finish, last, members), in_specs=[vmem]...]
where the time goes in v3:
time: 17.6 us; the launch traced here: 17.4 us
  Pallas kernels  17.4 us (99%)
    pallas_call x1, Pallas kernels, per_device(): pl.pallas_call(functools.partial(kernel, 'tok', members, tiles, last), in...  16 us
    pallas_call x1, Pallas kernels, per_device(): pl.pallas_call(functools.partial(finish, last, members), in_specs=[vmem]...  1.37 us

profile of v3, /device:TPU:16, one launch (start us, length us, event | category | flops | bytes accessed | tf_op | source)
XLA Modules:
  0.0 17.4 jit_solution(15047986233793421961)
XLA Ops:
  0.0 16.0 %shard_map.73 = (bf16[256,4096]{1,0:T(8,128)(2,1)S(1)}, bf16[8,128,512]{2,1,0:T(8,128)(2,1)S(1)}, bf16[8,64,512]{2,1,0:T(8,128)(2,1)S(1)}, bf16[8,4,256,256]{3,2...) custom-call(bf16[256,4096]{1,0:T(8,128)(2,1)} %q.1, ...), custom_call_target="tpu_custom_call" | custom-call | tf_op jit(solution)/shard_map/pallas_call | solution.py:342
  16.0 1.4 %shard_map.74 = bf16[256,4096]{1,0:T(8,128)(2,1)} custom-call(bf16[256,4096]{1,0:T(8,128)(2,1)S(1)} %get-tuple-element.12.done, bf16[8,128,512]{2,1,0:T(8,128)(2,1)S(1)} %get-tuple-element.13.halo, bf16[8,64,512]{2,1,0:T(8,128)(2,1)S(1)} %get-tuple-element.14.mids, bf16[8,4,256,256]{3,2,1,0:T(8,128)(2,1)S(1)} %get-tuple-element.15.tables, ...), custom_call_target="tpu_custom_call" | custom-call | tf_op jit(solution)/shard_map/pallas_call | solution.py:385

commit v4 on v3

--- a/solution.py
+++ b/solution.py
@@ -2,6 +2,7 @@
 
 import jax
 import jax.numpy as jnp
+import numpy as np
 from jax import lax
 from jax.experimental import pallas as pl
 from jax.experimental.pallas import tpu as pltpu
@@ -10,6 +11,8 @@
 LANES = 128
 TILE = 512
 LAST = 3
+DETOURS = 3
+HANDOVER = 5
 F32, BF16 = jnp.float32, jnp.bfloat16
 
 
@@ -43,12 +46,12 @@
     return (gate[c, n] * fresh + rest[c, n]).astype(BF16)
 
 
-def kernel(axis, members, tiles, last, q, k, v, seg_hbm, taps_hbm, filters_hbm, bias_hbm,
+def kernel(axis, members, tiles, last, detours, q, k, v, seg_hbm, taps_hbm, filters_hbm, bias_hbm,
            out, halo, mids, tables, gate, rest, emask,
            seg, taps, filters, bias, qb, kv, pt, raw, edge_send, edge, seg_prev,
            hrev, comb, biasf, segc, one, two, own_head, dmask, wide,
            small_sem, raw_sem, tail_sem, head_sem, q_sem,
-           send_sem, recv_sem, small_send, small_recv):
+           send_sem, recv_sem, small_send, small_recv, passing=None, pass_send=None, pass_recv=None, ready=None):
     rows, width = q.shape
     block = filters.shape[0]
     half = block // 2
@@ -59,11 +62,27 @@
     size = lax.axis_size(axis)
     has_left, has_right = me > 0, me < size - 1
     left, right = jnp.maximum(me - 1, 0), jnp.minimum(me + 1, size - 1)
+    turns = (me % 4 == 3) & (me // 4 < detours)
+    layer = jnp.minimum(me // 4, max(detours - 1, 0))
+    odd_one = tiles - 2
+    aside, along = pl.ds(0, tile // 2), pl.ds(tile // 2, tile // 2)
     barrier = pltpu.get_barrier_semaphore()
+
+    def greet(device):
+        pl.semaphore_signal(barrier, inc=1, device_id={axis: device}, device_id_type=pl.DeviceIdType.MESH)
 
     @pl.when(has_left)
     def _():
-        pl.semaphore_signal(barrier, inc=1, device_id={axis: left}, device_id_type=pl.DeviceIdType.MESH)
+        greet(left)
+
+    if detours:
+        lands = (me % 4 == 0) & (me > 0) & (me // 4 <= detours)
+
+        @pl.when(me == 0)
+        def _():
+            for z in range(detours):
+                greet(4 * z + 3)
+                greet(4 * z + 4)
 
     def cols(c):
         return pl.ds(pl.multiple_of(c * tile, tile), tile)
@@ -85,10 +104,24 @@
     def q_copy(c):
         return pltpu.make_async_copy(q.at[:, cols(c)], qb.at[c], q_sem.at[c])
 
-    def remote(src, dst, s, r):
+    def remote(src, dst, s, r, device=right):
         return pltpu.make_async_remote_copy(
             src_ref=src, dst_ref=dst, send_sem=s, recv_sem=r,
-            device_id={axis: right}, device_id_type=pl.DeviceIdType.MESH)
+            device_id={axis: device}, device_id_type=pl.DeviceIdType.MESH)
+
+    def along_copy():
+        return remote(pt.at[odd_one, :, along], halo.at[odd_one, :, along], send_sem.at[0], recv_sem.at[odd_one])
+
+    def aside_copy(z):
+        return remote(pt.at[odd_one, :, aside], passing.at[z], send_sem.at[0], pass_recv.at[z], 0)
+
+    def onward_copy(z):
+        return remote(passing.at[z], halo.at[odd_one, :, aside], pass_send.at[z], recv_sem.at[odd_one], 4 * z + 4)
+
+    def order(i):
+        if not detours:
+            return i
+        return jnp.where(turns, jnp.where(i == 0, odd_one, jnp.where(i <= odd_one, i - 1, i)), i)
 
     def product_copy(c):
         return remote(pt.at[c], halo.at[c], send_sem.at[0], recv_sem.at[c])
@@ -110,7 +143,8 @@
     small[1].start()
 
     @pl.loop(0, tiles)
-    def _(c):
+    def _(i):
+        c = order(i)
         tail_copy(0, c).start()
         tail_copy(1, c).start()
 
@@ -159,7 +193,8 @@
     small[1].wait()
 
     @pl.loop(0, tiles)
-    def _(c):
+    def _(step):
+        c = order(step)
         whole(kv.at[:, c, pl.ds(keep, rows - keep)], tail_sem.at[c]).wait()
         for s in range(0, tile, LANES):
             at, here = part(c, s), slice(s, s + LANES)
@@ -169,13 +204,34 @@
                 feats.append(feature(wide.at[i, s // LANES], x, 8, taps_of(i, at), block, block))
             pt[c, :, here] = (feats[0] * feats[1]).astype(BF16)
 
-        @pl.when(has_right & (c == 0))
+        @pl.when(has_right & (step == 0))
         def _():
-            pl.semaphore_wait(barrier, 1)
+            if detours:
+                pl.semaphore_wait(barrier, jnp.where(turns | lands, 2, 1))
+
+                @pl.when(lands)
+                def _():
+                    pl.semaphore_signal(
+                        ready, inc=1, device_id={axis: 0}, device_id_type=pl.DeviceIdType.MESH)
+
+            else:
+                pl.semaphore_wait(barrier, 1)
             seg_copy().start()
             edge_copy().start()
 
-        @pl.when(has_right)
+        if detours:
+            split = turns & (step == 0)
+
+            @pl.when(split)
+            def _():
+                aside_copy(layer).start()
+                along_copy().start()
+
+            straight = has_right & jnp.logical_not(split)
+        else:
+            straight = has_right
+
+        @pl.when(straight)
         def _():
             product_copy(c).start()
 
@@ -237,6 +293,14 @@
 
     @pl.loop(0, tiles)
     def _(c):
+        if detours:
+            @pl.when((me == 0) & (c == HANDOVER * tiles // 8))
+            def _():
+                pl.semaphore_wait(ready, detours)
+                for z in reversed(range(detours)):
+                    aside_copy(z).wait_recv()
+                    onward_copy(z).start()
+
         whole(kv.at[:, c, pl.ds(0, keep)], head_sem.at[c]).wait()
         q_copy(c).wait()
         for s in range(0, tile, LANES):
@@ -298,6 +362,12 @@
         seg_copy().wait_send()
         edge_copy().wait_send()
         remote(pt, halo, send_sem.at[0], recv_sem.at[0]).wait_send()
+
+    if detours:
+        @pl.when(me == 0)
+        def _():
+            for z in range(detours):
+                onward_copy(z).wait_send()
 
 
 def finish(last, members, done, halo, mids, tables, gate, rest, emask, out, fresh, sem):
@@ -327,7 +397,25 @@
         copy.wait()
 
 
-def per_device(queries, keys, values, segments, short_filters, mr_filter, mr_bias):
+def layers_of(mesh, axis):
+    at = mesh.axis_names.index(axis)
+    lines = np.moveaxis(mesh.devices, at, -1).reshape(-1, mesh.shape[axis])
+    if lines.shape[1] % 4:
+        return 1
+    for line in lines:
+        spots = [getattr(d, "coords", None) for d in line]
+        if None in spots:
+            return 1
+        spots = np.array([tuple(spot) for spot in spots])
+        spots = spots - spots[0]
+        chip = np.arange(len(line)) // 2
+        want = np.stack([np.zeros_like(chip), chip % 2, chip // 2], 1)
+        if not np.array_equal(spots, want):
+            return 1
+    return lines.shape[1] // 4
+
+
+def per_device(layers, queries, keys, values, segments, short_filters, mr_filter, mr_bias):
     rows, width = queries.shape
     block, groups = mr_filter.shape
     half = block // 2
@@ -338,9 +426,10 @@
     dma = pltpu.SemaphoreType.DMA
     chunked = lambda r: pltpu.VMEM((tiles, r, tile), BF16)
     last = min(LAST, tiles)
+    detours = min(DETOURS, layers - 1) if tiles > 1 else 0
     vmem = pl.BlockSpec(memory_space=pltpu.VMEM)
     held = pl.pallas_call(
-        functools.partial(kernel, "tok", members, tiles, last),
+        functools.partial(kernel, "tok", members, tiles, last, detours),
         in_specs=[pl.BlockSpec(memory_space=pltpu.HBM)] * 7,
         out_specs=[vmem] * 7,
         out_shape=[
@@ -375,7 +464,10 @@
             pltpu.VMEM((3, parts, rows + 8, LANES), F32),
             dma((4,)), dma((1,)), dma((tiles,)), dma((tiles,)), dma((tiles,)),
             dma((1,)), dma((tiles,)), dma((2,)), dma((2,)),
-        ],
+        ] + ([
+            pltpu.VMEM((detours, block, tile // 2), BF16), dma((detours,)), dma((detours,)),
+            pltpu.SemaphoreType.REGULAR,
+        ] if detours else []),
         compiler_params=pltpu.CompilerParams(
             collective_id=0, has_side_effects=True, vmem_limit_bytes=24 * 2**20
         ),
@@ -403,5 +495,5 @@
         P(),
     )
     return jax.shard_map(
-        per_device, mesh=mesh, in_specs=placed, out_specs=P(("seq", "tok"), None), check_vma=False
+        functools.partial(per_device, layers_of(mesh, "tok")), mesh=mesh, in_specs=placed, out_specs=P(("seq", "tok"), None), check_vma=False
     )

time: 17.6 us -> 16.9 us (0.960)
  Pallas kernels: 17.4 us -> 16.8 us
    pallas_call x1, Pallas kernels: 16 us -> 15.4 us  [per_device(): pl.pallas_call(functools.partial(kernel, 'tok', members, tiles, last, det...]
where the time goes in v4:
time: 16.9 us; the launch traced here: 16.8 us
  Pallas kernels  16.8 us (99%)
    pallas_call x1, Pallas kernels, per_device(): pl.pallas_call(functools.partial(kernel, 'tok', members, tiles, last, det...  15.4 us
    pallas_call x1, Pallas kernels, per_device(): pl.pallas_call(functools.partial(finish, last, members), in_specs=[vmem]...  1.37 us

profile of v4, /device:TPU:16, one launch (start us, length us, event | category | flops | bytes accessed | tf_op | source)
XLA Modules:
  0.0 16.8 jit_solution(18095322103931913966)
XLA Ops:
  0.0 15.4 %shard_map.73 = (bf16[256,4096]{1,0:T(8,128)(2,1)S(1)}, bf16[8,128,512]{2,1,0:T(8,128)(2,1)S(1)}, bf16[8,64,512]{2,1,0:T(8,128)(2,1)S(1)}, bf16[8,4,256,256]{3,2...) custom-call(bf16[256,4096]{1,0:T(8,128)(2,1)} %q.1, ...), custom_call_target="tpu_custom_call" | custom-call | tf_op jit(solution)/shard_map/pallas_call | solution.py:431
  15.4 1.4 %shard_map.74 = bf16[256,4096]{1,0:T(8,128)(2,1)} custom-call(bf16[256,4096]{1,0:T(8,128)(2,1)S(1)} %get-tuple-element.12.done, bf16[8,128,512]{2,1,0:T(8,128)(2,1)S(1)} %get-tuple-element.13.halo, bf16[8,64,512]{2,1,0:T(8,128)(2,1)S(1)} %get-tuple-element.14.mids, bf16[8,4,256,256]{3,2,1,0:T(8,128)(2,1)S(1)} %get-tuple-element.15.tables, ...), custom_call_target="tpu_custom_call" | custom-call | tf_op jit(solution)/shard_map/pallas_call | solution.py:477

commit v5 on v4

--- a/solution.py
+++ b/solution.py
@@ -18,6 +18,11 @@
 
 def column(row, block):
     return jnp.transpose(jnp.broadcast_to(row, (block, block)))
+
+
+def cuts_of(tiles, last):
+    inner = tiles - last
+    return [0] + [n for n in (1, 3) if n < inner] + ([inner] if inner else []) + [tiles]
 
 
 def quads(half, members):
@@ -48,7 +53,7 @@
 
 def kernel(axis, members, tiles, last, detours, q, k, v, seg_hbm, taps_hbm, filters_hbm, bias_hbm,
            out, halo, mids, tables, gate, rest, emask,
-           seg, taps, filters, bias, qb, kv, pt, raw, edge_send, edge, seg_prev,
+           seg, taps, filters, bias, qb, kv, pt, raw, edge_send, edge,
            hrev, comb, biasf, segc, one, two, own_head, dmask, wide,
            small_sem, raw_sem, tail_sem, head_sem, q_sem,
            send_sem, recv_sem, small_send, small_recv, passing=None, pass_send=None, pass_recv=None, ready=None):
@@ -64,8 +69,10 @@
     left, right = jnp.maximum(me - 1, 0), jnp.minimum(me + 1, size - 1)
     turns = (me % 4 == 3) & (me // 4 < detours)
     layer = jnp.minimum(me // 4, max(detours - 1, 0))
-    odd_one = tiles - 2
-    aside, along = pl.ds(0, tile // 2), pl.ds(tile // 2, tile // 2)
+    cuts = cuts_of(tiles, last)
+    odd_one = cuts[-2]
+    wide_part = tile // 4 * 3
+    aside, along = pl.ds(0, wide_part), pl.ds(wide_part, tile - wide_part)
     barrier = pltpu.get_barrier_semaphore()
 
     def greet(device):
@@ -110,27 +117,23 @@
             device_id={axis: device}, device_id_type=pl.DeviceIdType.MESH)
 
     def along_copy():
-        return remote(pt.at[odd_one, :, along], halo.at[odd_one, :, along], send_sem.at[0], recv_sem.at[odd_one])
+        return remote(pt.at[odd_one, :, along], halo.at[odd_one, :, along], send_sem.at[0], recv_sem.at[len(cuts) - 2])
 
     def aside_copy(z):
         return remote(pt.at[odd_one, :, aside], passing.at[z], send_sem.at[0], pass_recv.at[z], 0)
 
     def onward_copy(z):
-        return remote(passing.at[z], halo.at[odd_one, :, aside], pass_send.at[z], recv_sem.at[odd_one], 4 * z + 4)
+        return remote(passing.at[z], halo.at[odd_one, :, aside], pass_send.at[z], recv_sem.at[len(cuts) - 2], 4 * z + 4)
 
     def order(i):
-        if not detours:
-            return i
-        return jnp.where(turns, jnp.where(i == 0, odd_one, jnp.where(i <= odd_one, i - 1, i)), i)
-
-    def product_copy(c):
-        return remote(pt.at[c], halo.at[c], send_sem.at[0], recv_sem.at[c])
+        return jnp.where(i == 0, odd_one, jnp.where(i <= odd_one, i - 1, i))
+
+    def part_copy(g, skip=0):
+        at = pl.ds(cuts[g] + skip, cuts[g + 1] - cuts[g] - skip)
+        return remote(pt.at[at], halo.at[at], send_sem.at[0], recv_sem.at[g])
 
     def edge_copy():
         return remote(edge_send, edge, small_send.at[0], small_recv.at[0])
-
-    def seg_copy():
-        return remote(seg, seg_prev, small_send.at[1], small_recv.at[1])
 
     small = [
         pltpu.make_async_copy(src, dst, small_sem.at[i])
@@ -182,7 +185,10 @@
     short_masks(block, block)
     whole(raw, raw_sem.at[0]).wait()
     for i in range(3):
-        edge_send[i] = raw[i].astype(F32)[6:8].astype(BF16)
+        edge_send[i, :, :width] = raw[i].astype(F32)[6:8].astype(BF16)
+    edge_send[0, :, width:] = jnp.broadcast_to(seg[1:2].astype(F32), (2, block)).astype(BF16)
+    for i in (1, 2):
+        edge_send[i, :, width:] = jnp.zeros((2, block), BF16)
 
     def part(c, s):
         return pl.ds(pl.multiple_of(c * tile + s, LANES), LANES)
@@ -192,8 +198,7 @@
 
     small[1].wait()
 
-    @pl.loop(0, tiles)
-    def _(step):
+    def produce(step):
         c = order(step)
         whole(kv.at[:, c, pl.ds(keep, rows - keep)], tail_sem.at[c]).wait()
         for s in range(0, tile, LANES):
@@ -204,36 +209,45 @@
                 feats.append(feature(wide.at[i, s // LANES], x, 8, taps_of(i, at), block, block))
             pt[c, :, here] = (feats[0] * feats[1]).astype(BF16)
 
-        @pl.when(has_right & (step == 0))
+    def open_link():
+        if not detours:
+            pl.semaphore_wait(barrier, 1)
+            edge_copy().start()
+            return
+        pl.semaphore_wait(barrier, jnp.where(turns | lands, 2, 1))
+        edge_copy().start()
+
+        @pl.when(lands)
         def _():
-            if detours:
-                pl.semaphore_wait(barrier, jnp.where(turns | lands, 2, 1))
-
-                @pl.when(lands)
-                def _():
-                    pl.semaphore_signal(
-                        ready, inc=1, device_id={axis: 0}, device_id_type=pl.DeviceIdType.MESH)
-
-            else:
-                pl.semaphore_wait(barrier, 1)
-            seg_copy().start()
-            edge_copy().start()
-
-        if detours:
-            split = turns & (step == 0)
-
-            @pl.when(split)
+            pl.semaphore_signal(ready, inc=1, device_id={axis: 0}, device_id_type=pl.DeviceIdType.MESH)
+
+        @pl.when(turns)
+        def _():
+            aside_copy(layer).start()
+            along_copy().start()
+
+    begin = 0
+    for g in range(len(cuts) - 1):
+        final = g == len(cuts) - 2
+        end = tiles if final else cuts[g + 1] + 1
+        pl.loop(begin, end)(produce)
+        begin = end
+
+        @pl.when(has_right)
+        def _():
+            if g == 0:
+                open_link()
+            if not (final and detours):
+                part_copy(g).start()
+                return
+
+            @pl.when(turns)
             def _():
-                aside_copy(layer).start()
-                along_copy().start()
-
-            straight = has_right & jnp.logical_not(split)
-        else:
-            straight = has_right
-
-        @pl.when(straight)
-        def _():
-            product_copy(c).start()
+                part_copy(g, 1).start()
+
+            @pl.when(jnp.logical_not(turns))
+            def _():
+                part_copy(g).start()
 
     small[2].wait()
     small[3].wait()
@@ -272,19 +286,17 @@
 
     @pl.when(has_left)
     def _():
-        seg_copy().wait_recv()
         edge_copy().wait_recv()
 
     @pl.when(jnp.logical_not(has_left))
     def _():
-        seg_prev[...] = jnp.zeros_like(seg_prev)
         edge[...] = jnp.zeros_like(edge)
 
         @pl.loop(0, tiles)
         def _(c):
             halo[c] = jnp.zeros_like(halo[c])
 
-    segc[pl.ds(0, block)] = column(seg_prev[1:2].astype(F32), block)
+    segc[pl.ds(0, block)] = column(edge[0, :, width:].astype(F32)[0:1], block)
     short_masks(0, block)
     early_masks(0)
     early_masks(1)
@@ -341,25 +353,23 @@
             out[block:, at] = (fq[block:] * (sure1 + fresh * own_head[pl.ds(block, block)])).astype(BF16)
             mids[c, :, here] = mid[:half]
 
-    def arrive(c):
-        @pl.when(has_left)
-        def _():
-            product_copy(c).wait_recv()
-
     @pl.loop(0, tiles - last)
     def _(c):
-        arrive(c)
+        for g in range(len(cuts) - 2):
+            @pl.when(has_left & (c == cuts[g]))
+            def _():
+                part_copy(g).wait_recv()
+
         for s in range(0, tile, LANES):
             out[:block, part(c, s)] = join(
                 c, s // LANES, slice(s, s + LANES), halo, mids, tables, gate, rest, emask.at[0:2], quad)
 
-    @pl.loop(tiles - last, tiles)
-    def _(c):
-        arrive(c)
+    @pl.when(has_left)
+    def _():
+        part_copy(len(cuts) - 2).wait_recv()
 
     @pl.when(has_right)
     def _():
-        seg_copy().wait_send()
         edge_copy().wait_send()
         remote(pt, halo, send_sem.at[0], recv_sem.at[0]).wait_send()
 
@@ -450,9 +460,8 @@
             pltpu.VMEM((2, tiles, rows, tile), BF16),
             chunked(block),
             pltpu.VMEM((3, 8, width), BF16),
-            pltpu.VMEM((3, 2, width), BF16),
-            pltpu.VMEM((3, 2, width), BF16),
-            pltpu.VMEM((rows // block, block), jnp.int32),
+            pltpu.VMEM((3, 2, width + block), BF16),
+            pltpu.VMEM((3, 2, width + block), BF16),
             pltpu.VMEM((groups, block), F32),
             pltpu.VMEM((groups, block), F32),
             pltpu.VMEM((width // LANES, LANES), F32),
@@ -463,9 +472,9 @@
             pltpu.VMEM((4, half, LANES), BF16),
             pltpu.VMEM((3, parts, rows + 8, LANES), F32),
             dma((4,)), dma((1,)), dma((tiles,)), dma((tiles,)), dma((tiles,)),
-            dma((1,)), dma((tiles,)), dma((2,)), dma((2,)),
+            dma((1,)), dma((len(cuts_of(tiles, last)) - 1,)), dma((1,)), dma((1,)),
         ] + ([
-            pltpu.VMEM((detours, block, tile // 2), BF16), dma((detours,)), dma((detours,)),
+            pltpu.VMEM((detours, block, tile // 4 * 3), BF16), dma((detours,)), dma((detours,)),
             pltpu.SemaphoreType.REGULAR,
         ] if detours else []),
         compiler_params=pltpu.CompilerParams(

time: 16.9 us -> 16.8 us (level); the launches traced: 16.8 us -> 16.5 us
  Pallas kernels: 16.8 us -> 16.5 us
    pallas_call x1, Pallas kernels: 15.4 us -> 15.1 us  [per_device(): pl.pallas_call(functools.partial(kernel, 'tok', members, tiles, last, det...]
where the time goes in v5:
time: 16.8 us; the launch traced here: 16.5 us
  Pallas kernels  16.5 us (98%)
    pallas_call x1, Pallas kernels, per_device(): pl.pallas_call(functools.partial(kernel, 'tok', members, tiles, last, det...  15.1 us
    pallas_call x1, Pallas kernels, per_device(): pl.pallas_call(functools.partial(finish, last, members), in_specs=[vmem]...  1.37 us

profile of v5, /device:TPU:16, one launch (start us, length us, event | category | flops | bytes accessed | tf_op | source)
XLA Modules:
  0.0 16.5 jit_solution(15944281093118401506)
XLA Ops:
  0.0 15.1 %shard_map.73 = (bf16[256,4096]{1,0:T(8,128)(2,1)S(1)}, bf16[8,128,512]{2,1,0:T(8,128)(2,1)S(1)}, bf16[8,64,512]{2,1,0:T(8,128)(2,1)S(1)}, bf16[8,4,256,256]{3,2...) custom-call(bf16[256,4096]{1,0:T(8,128)(2,1)} %q.1, ...), custom_call_target="tpu_custom_call" | custom-call | tf_op jit(solution)/shard_map/pallas_call | solution.py:441
  15.1 1.4 %shard_map.74 = bf16[256,4096]{1,0:T(8,128)(2,1)} custom-call(bf16[256,4096]{1,0:T(8,128)(2,1)S(1)} %get-tuple-element.12.done, bf16[8,128,512]{2,1,0:T(8,128)(2,1)S(1)} %get-tuple-element.13.halo, bf16[8,64,512]{2,1,0:T(8,128)(2,1)S(1)} %get-tuple-element.14.mids, bf16[8,4,256,256]{3,2,1,0:T(8,128)(2,1)S(1)} %get-tuple-element.15.tables, ...), custom_call_target="tpu_custom_call" | custom-call | tf_op jit(solution)/shard_map/pallas_call | solution.py:486

commit v6 on v5

--- a/solution.py
+++ b/solution.py
@@ -22,7 +22,7 @@
 
 def cuts_of(tiles, last):
     inner = tiles - last
-    return [0] + [n for n in (1, 3) if n < inner] + ([inner] if inner else []) + [tiles]
+    return [0] + [n for n in (1,) if n < inner] + ([inner] if inner else []) + [tiles]
 
 
 def quads(half, members):
@@ -221,11 +221,8 @@
         def _():
             pl.semaphore_signal(ready, inc=1, device_id={axis: 0}, device_id_type=pl.DeviceIdType.MESH)
 
-        @pl.when(turns)
-        def _():
-            aside_copy(layer).start()
-            along_copy().start()
-
+
+    pl.when(has_right)(open_link)
     begin = 0
     for g in range(len(cuts) - 1):
         final = g == len(cuts) - 2
@@ -235,8 +232,12 @@
 
         @pl.when(has_right)
         def _():
-            if g == 0:
-                open_link()
+            if g == 0 and detours:
+                @pl.when(turns)
+                def _():
+                    aside_copy(layer).start()
+                    along_copy().start()
+
             if not (final and detours):
                 part_copy(g).start()
                 return

time: 16.8 us -> 16.8 us (level)
  no operation moved by 1% of the time
where the time goes in v6:
time: 16.8 us; the launch traced here: 16.5 us
  Pallas kernels  16.5 us (98%)
    pallas_call x1, Pallas kernels, per_device(): pl.pallas_call(functools.partial(kernel, 'tok', members, tiles, last, det...  15.1 us
    pallas_call x1, Pallas kernels, per_device(): pl.pallas_call(functools.partial(finish, last, members), in_specs=[vmem]...  1.37 us

profile of v6, /device:TPU:16, one launch (start us, length us, event | category | flops | bytes accessed | tf_op | source)
XLA Modules:
  0.0 16.5 jit_solution(13501444712374942719)
XLA Ops:
  0.0 15.1 %shard_map.73 = (bf16[256,4096]{1,0:T(8,128)(2,1)S(1)}, bf16[8,128,512]{2,1,0:T(8,128)(2,1)S(1)}, bf16[8,64,512]{2,1,0:T(8,128)(2,1)S(1)}, bf16[8,4,256,256]{3,2...) custom-call(bf16[256,4096]{1,0:T(8,128)(2,1)} %q.1, ...), custom_call_target="tpu_custom_call" | custom-call | tf_op jit(solution)/shard_map/pallas_call | solution.py:442
  15.1 1.4 %shard_map.74 = bf16[256,4096]{1,0:T(8,128)(2,1)} custom-call(bf16[256,4096]{1,0:T(8,128)(2,1)S(1)} %get-tuple-element.12.done, bf16[8,128,512]{2,1,0:T(8,128)(2,1)S(1)} %get-tuple-element.13.halo, bf16[8,64,512]{2,1,0:T(8,128)(2,1)S(1)} %get-tuple-element.14.mids, bf16[8,4,256,256]{3,2,1,0:T(8,128)(2,1)S(1)} %get-tuple-element.15.tables, ...), custom_call_target="tpu_custom_call" | custom-call | tf_op jit(solution)/shard_map/pallas_call | solution.py:487

commit v7 on v6

--- a/solution.py
+++ b/solution.py
@@ -70,6 +70,8 @@
     turns = (me % 4 == 3) & (me // 4 < detours)
     layer = jnp.minimum(me // 4, max(detours - 1, 0))
     cuts = cuts_of(tiles, last)
+    ends = [n + 1 for n in cuts[1:-1]] + [tiles]
+    soon = min(2, tiles - 1)
     odd_one = cuts[-2]
     wide_part = tile // 4 * 3
     aside, along = pl.ds(0, wide_part), pl.ds(wide_part, tile - wide_part)
@@ -97,19 +99,19 @@
     def raw_copy(i):
         return pltpu.make_async_copy((q, k, v)[i].at[pl.ds(rows - 8, 8)], raw.at[i], raw_sem.at[0])
 
-    def tail_copy(i, c):
+    def tail_copy(i, c, g):
         at = pl.ds(keep, rows - keep)
-        return pltpu.make_async_copy((k, v)[i].at[at, cols(c)], kv.at[i, c, at], tail_sem.at[c])
+        return pltpu.make_async_copy((k, v)[i].at[at, cols(c)], kv.at[i, c, at], tail_sem.at[g])
 
     def head_copy(i, c):
         at = pl.ds(0, keep)
-        return pltpu.make_async_copy((k, v)[i].at[at, cols(c)], kv.at[i, c, at], head_sem.at[c])
+        return pltpu.make_async_copy((k, v)[i].at[at, cols(c)], kv.at[i, c, at], head_sem.at[jnp.where(c < soon, 0, 1)])
 
     def whole(ref, sem):
         return pltpu.make_async_copy(ref, ref, sem)
 
     def q_copy(c):
-        return pltpu.make_async_copy(q.at[:, cols(c)], qb.at[c], q_sem.at[c])
+        return pltpu.make_async_copy(q.at[:, cols(c)], qb.at[c], q_sem.at[jnp.where(c < soon, 0, 1)])
 
     def remote(src, dst, s, r, device=right):
         return pltpu.make_async_remote_copy(
@@ -120,10 +122,10 @@
         return remote(pt.at[odd_one, :, along], halo.at[odd_one, :, along], send_sem.at[0], recv_sem.at[len(cuts) - 2])
 
     def aside_copy(z):
-        return remote(pt.at[odd_one, :, aside], passing.at[z], send_sem.at[0], pass_recv.at[z], 0)
+        return remote(pt.at[odd_one, :, aside], passing.at[z], send_sem.at[0], pass_recv.at[0], 0)
 
     def onward_copy(z):
-        return remote(passing.at[z], halo.at[odd_one, :, aside], pass_send.at[z], recv_sem.at[len(cuts) - 2], 4 * z + 4)
+        return remote(passing.at[z], halo.at[odd_one, :, aside], pass_send.at[0], recv_sem.at[len(cuts) - 2], 4 * z + 4)
 
     def order(i):
         return jnp.where(i == 0, odd_one, jnp.where(i <= odd_one, i - 1, i))
@@ -148,8 +150,9 @@
     @pl.loop(0, tiles)
     def _(i):
         c = order(i)
-        tail_copy(0, c).start()
-        tail_copy(1, c).start()
+        g = sum((i >= n).astype(jnp.int32) for n in ends[:-1])
+        tail_copy(0, c, g).start()
+        tail_copy(1, c, g).start()
 
     small[2].start()
     small[3].start()
@@ -200,7 +203,6 @@
 
     def produce(step):
         c = order(step)
-        whole(kv.at[:, c, pl.ds(keep, rows - keep)], tail_sem.at[c]).wait()
         for s in range(0, tile, LANES):
             at, here = part(c, s), slice(s, s + LANES)
             feats = []
@@ -226,7 +228,8 @@
     begin = 0
     for g in range(len(cuts) - 1):
         final = g == len(cuts) - 2
-        end = tiles if final else cuts[g + 1] + 1
+        end = ends[g]
+        whole(kv.at[:, pl.ds(begin, end - begin), pl.ds(keep, rows - keep)], tail_sem.at[g]).wait()
         pl.loop(begin, end)(produce)
         begin = end
 
@@ -310,12 +313,16 @@
             @pl.when((me == 0) & (c == HANDOVER * tiles // 8))
             def _():
                 pl.semaphore_wait(ready, detours)
+                whole(passing, pass_recv.at[0]).wait()
                 for z in reversed(range(detours)):
-                    aside_copy(z).wait_recv()
                     onward_copy(z).start()
 
-        whole(kv.at[:, c, pl.ds(0, keep)], head_sem.at[c]).wait()
-        q_copy(c).wait()
+        for g, (a, b) in enumerate(((0, soon), (soon, tiles))):
+            @pl.when(c == a)
+            def _():
+                whole(kv.at[:, pl.ds(a, b - a), pl.ds(0, keep)], head_sem.at[g]).wait()
+                whole(qb.at[pl.ds(a, b - a)], q_sem.at[g]).wait()
+
         for s in range(0, tile, LANES):
             at, here, n = part(c, s), slice(s, s + LANES), s // LANES
 
@@ -377,8 +384,7 @@
     if detours:
         @pl.when(me == 0)
         def _():
-            for z in range(detours):
-                onward_copy(z).wait_send()
+            whole(passing, pass_send.at[0]).wait()
 
 
 def finish(last, members, done, halo, mids, tables, gate, rest, emask, out, fresh, sem):
@@ -472,10 +478,10 @@
             pltpu.VMEM((rows, LANES), F32),
             pltpu.VMEM((4, half, LANES), BF16),
             pltpu.VMEM((3, parts, rows + 8, LANES), F32),
-            dma((4,)), dma((1,)), dma((tiles,)), dma((tiles,)), dma((tiles,)),
+            dma((4,)), dma((1,)), dma((len(cuts_of(tiles, last)) - 1,)), dma((2,)), dma((2,)),
             dma((1,)), dma((len(cuts_of(tiles, last)) - 1,)), dma((1,)), dma((1,)),
         ] + ([
-            pltpu.VMEM((detours, block, tile // 4 * 3), BF16), dma((detours,)), dma((detours,)),
+            pltpu.VMEM((detours, block, tile // 4 * 3), BF16), dma((1,)), dma((1,)),
             pltpu.SemaphoreType.REGULAR,
         ] if detours else []),
         compiler_params=pltpu.CompilerParams(

time: 16.8 us -> 16.7 us (level)
  no operation moved by 1% of the time
where the time goes in v7:
time: 16.7 us; the launch traced here: 16.4 us
  Pallas kernels  16.4 us (98%)
    pallas_call x1, Pallas kernels, per_device(): pl.pallas_call(functools.partial(kernel, 'tok', members, tiles, last, det...  15 us
    pallas_call x1, Pallas kernels, per_device(): pl.pallas_call(functools.partial(finish, last, members), in_specs=[vmem]...  1.37 us

profile of v7, /device:TPU:16, one launch (start us, length us, event | category | flops | bytes accessed | tf_op | source)
XLA Modules:
  0.0 16.4 jit_solution(16317958807733512977)
XLA Ops:
  0.0 15.0 %shard_map.73 = (bf16[256,4096]{1,0:T(8,128)(2,1)S(1)}, bf16[8,128,512]{2,1,0:T(8,128)(2,1)S(1)}, bf16[8,64,512]{2,1,0:T(8,128)(2,1)S(1)}, bf16[8,4,256,256]{3,2...) custom-call(bf16[256,4096]{1,0:T(8,128)(2,1)} %q.1, ...), custom_call_target="tpu_custom_call" | custom-call | tf_op jit(solution)/shard_map/pallas_call | solution.py:448
  15.1 1.4 %shard_map.74 = bf16[256,4096]{1,0:T(8,128)(2,1)} custom-call(bf16[256,4096]{1,0:T(8,128)(2,1)S(1)} %get-tuple-element.12.done, bf16[8,128,512]{2,1,0:T(8,128)(2,1)S(1)} %get-tuple-element.13.halo, bf16[8,64,512]{2,1,0:T(8,128)(2,1)S(1)} %get-tuple-element.14.mids, bf16[8,4,256,256]{3,2,1,0:T(8,128)(2,1)S(1)} %get-tuple-element.15.tables, ...), custom_call_target="tpu_custom_call" | custom-call | tf_op jit(solution)/shard_map/pallas_call | solution.py:493

commit v8 on v7

--- a/solution.py
+++ b/solution.py
@@ -394,11 +394,10 @@
     quad = quads(half, members)
     ready = width - last * tile
     copies = [
-        pltpu.make_async_copy(done.at[at], out.at[at], sem.at[i])
-        for i, at in enumerate((
+        pltpu.make_async_copy(done.at[at], out.at[at], sem.at[0])
+        for at in (
             (pl.ds(0, block), pl.ds(0, ready)),
-            (pl.ds(block, half), slice(None)),
-            (pl.ds(block + half, half), slice(None))))]
+            (pl.ds(block, rows - block), slice(None)))]
     for copy in copies:
         copy.start()
     for i in range(last):
@@ -407,11 +406,9 @@
             here = slice(s, s + LANES)
             fresh[i, :, here] = join(c, s // LANES, here, halo, mids, tables, gate, rest, emask.at[0:2], quad)
         copy = pltpu.make_async_copy(
-            fresh.at[i], out.at[pl.ds(0, block), pl.ds(ready + i * tile, tile)], sem.at[3 + i])
+            fresh.at[i], out.at[pl.ds(0, block), pl.ds(ready + i * tile, tile)], sem.at[0])
         copy.start()
-        copies.append(copy)
-    for copy in copies:
-        copy.wait()
+    pltpu.make_async_copy(done, out, sem.at[0]).wait()
 
 
 def layers_of(mesh, axis):
@@ -495,7 +492,7 @@
         in_specs=[vmem] * 7,
         out_specs=pl.BlockSpec(memory_space=pltpu.HBM),
         out_shape=pltpu.HBM((rows, width), BF16),
-        scratch_shapes=[pltpu.VMEM((last, block, tile), BF16), dma((3 + last,))],
+        scratch_shapes=[pltpu.VMEM((last, block, tile), BF16), dma((1,))],
         compiler_params=pltpu.CompilerParams(vmem_limit_bytes=8 * 2**20),
     )(*(pltpu.with_memory_space_constraint(x, pltpu.VMEM) for x in held))
 

time: 16.7 us -> 16.6 us (level)
  no operation moved by 1% of the time
where the time goes in v8:
time: 16.6 us; the launch traced here: 16.4 us
  Pallas kernels  16.4 us (99%)
    pallas_call x1, Pallas kernels, per_device(): pl.pallas_call(functools.partial(kernel, 'tok', members, tiles, last, det...  15 us
    pallas_call x1, Pallas kernels, per_device(): pl.pallas_call(functools.partial(finish, last, members), in_specs=[vmem]...  1.32 us

profile of v8, /device:TPU:16, one launch (start us, length us, event | category | flops | bytes accessed | tf_op | source)
XLA Modules:
  0.0 16.4 jit_solution(16082466493599223686)
XLA Ops:
  0.0 15.0 %shard_map.73 = (bf16[256,4096]{1,0:T(8,128)(2,1)S(1)}, bf16[8,128,512]{2,1,0:T(8,128)(2,1)S(1)}, bf16[8,64,512]{2,1,0:T(8,128)(2,1)S(1)}, bf16[8,4,256,256]{3,2...) custom-call(bf16[256,4096]{1,0:T(8,128)(2,1)} %q.1, ...), custom_call_target="tpu_custom_call" | custom-call | tf_op jit(solution)/shard_map/pallas_call | solution.py:445
  15.1 1.3 %shard_map.74 = bf16[256,4096]{1,0:T(8,128)(2,1)} custom-call(bf16[256,4096]{1,0:T(8,128)(2,1)S(1)} %get-tuple-element.12.done, bf16[8,128,512]{2,1,0:T(8,128)(2,1)S(1)} %get-tuple-element.13.halo, bf16[8,64,512]{2,1,0:T(8,128)(2,1)S(1)} %get-tuple-element.14.mids, bf16[8,4,256,256]{3,2,1,0:T(8,128)(2,1)S(1)} %get-tuple-element.15.tables, ...), custom_call_target="tpu_custom_call" | custom-call | tf_op jit(solution)/shard_map/pallas_call | solution.py:490
